TPU v7x, 32 devices: a whole 2x2x4 slice. The times are simulated.
32 devices in a mesh: dp: 16 (over z, y, core), space: 2 (over x).
Axes of the slice: x: 2, y: 2, z: 4, core: 2. Of those that a mesh axis runs over, the one named last changes fastest.
Arguments:
- volumes: bfloat16 [16, 32, 8, 8, 128], P('dp', None, 'space'), may hold values from -6 to 6
- w_first: bfloat16 [864, 64], P('dp'), may hold values from -0.21875 to 0.21875
- w_second: bfloat16 [1728, 128], P('dp'), may hold values from -0.4375 to 0.4375
- cotangent: bfloat16 [16, 128, 2, 2, 32], P('dp', None, 'space'), may hold values from -96 to 96
Outputs:
- pooled: bfloat16 [16, 128, 2, 2, 32], P('dp', None, 'space')
- volume_grad: bfloat16 [16, 32, 8, 8, 128], P('dp', None, 'space')
- grad_first: float32 [864, 64], P('dp')
- grad_second: float32 [1728, 128], P('dp')
All inputs are finite; a program needn't handle non-finite values.
Results may differ from a plain program's by a relative error of at most 0.023.
Values may be sent and summed in bfloat16 or wider, within the bound.
No kernel may reach another device: no remote copies, remote signals or barrier semaphores. Data moves between devices by JAX's collectives and lax.ppermute only.
A program may use at most 128 MiB of HBM per device.

v0:
```python
import jax
import jax.numpy as jnp
from jax import lax
from jax.sharding import PartitionSpec as P


def with_halo(block, sides, width):
    for axis, dim in sides:
        count = lax.axis_size(axis)
        forward = [(i, i + 1) for i in range(count - 1)]
        backward = [(target, source) for source, target in forward]
        low = lax.ppermute(
            lax.slice_in_dim(block, block.shape[dim] - width, None, axis=dim), axis, forward
        )
        high = lax.ppermute(lax.slice_in_dim(block, 0, width, axis=dim), axis, backward)
        block = jnp.concatenate([low, block, high], axis=dim)
    return block


def pad_sides(field):
    return jnp.pad(field, ((0, 0), (0, 0), (0, 0), (1, 1), (1, 1)))


def conv_forward(padded, weight):
    samples_here, in_width, depth_padded, extent_y, extent_z = padded.shape
    extent_x = depth_padded - 2
    out_width = weight.shape[1]
    framed = pad_sides(padded)
    kernel = weight.reshape(3, 3, 3, in_width, out_width)
    summed = jnp.zeros((samples_here, out_width, extent_x, extent_y, extent_z), jnp.float32)
    for along_x in range(3):
        for along_y in range(3):
            for along_z in range(3):
                window = framed[
                    :,
                    :,
                    along_x : along_x + extent_x,
                    along_y : along_y + extent_y,
                    along_z : along_z + extent_z,
                ]
                summed = summed + jnp.einsum(
                    "sixyz,io->soxyz",
                    window,
                    kernel[along_x, along_y, along_z],
                    preferred_element_type=jnp.float32,
                )
    return summed


def conv_input_grad(padded, weight, in_width):
    samples_here, out_width, depth_padded, extent_y, extent_z = padded.shape
    extent_x = depth_padded - 2
    framed = pad_sides(padded)
    kernel = weight.reshape(3, 3, 3, in_width, out_width)
    summed = jnp.zeros((samples_here, in_width, extent_x, extent_y, extent_z), jnp.float32)
    for along_x in range(3):
        for along_y in range(3):
            for along_z in range(3):
                window = framed[
                    :,
                    :,
                    2 - along_x : 2 - along_x + extent_x,
                    2 - along_y : 2 - along_y + extent_y,
                    2 - along_z : 2 - along_z + extent_z,
                ]
                summed = summed + jnp.einsum(
                    "soxyz,io->sixyz",
                    window,
                    kernel[along_x, along_y, along_z],
                    preferred_element_type=jnp.float32,
                )
    return summed


def conv_weight_grad(padded, grads):
    samples_here, in_width, depth_padded, extent_y, extent_z = padded.shape
    extent_x = depth_padded - 2
    framed = pad_sides(padded)
    pieces = []
    for along_x in range(3):
        for along_y in range(3):
            for along_z in range(3):
                window = framed[
                    :,
                    :,
                    along_x : along_x + extent_x,
                    along_y : along_y + extent_y,
                    along_z : along_z + extent_z,
                ]
                pieces.append(
                    jnp.einsum("sixyz,soxyz->io", window, grads, preferred_element_type=jnp.float32)
                )
    return jnp.stack(pieces).reshape(27 * in_width, grads.shape[1])


def pooling(field):
    samples_here, width, extent_x, extent_y, extent_z = field.shape
    blocks = field.reshape(
        samples_here, width, extent_x // 2, 2, extent_y // 2, 2, extent_z // 2, 2
    )
    return jnp.mean(blocks, axis=(3, 5, 7))


def spread_up(field):
    samples_here, width, extent_x, extent_y, extent_z = field.shape
    blocks = jnp.broadcast_to(
        field[:, :, :, None, :, None, :, None],
        (samples_here, width, extent_x, 2, extent_y, 2, extent_z, 2),
    )
    return blocks.reshape(samples_here, width, 2 * extent_x, 2 * extent_y, 2 * extent_z)


def silu_slope(values):
    sigma = jax.nn.sigmoid(values)
    return sigma * (1.0 + values * (1.0 - sigma))


def local(volumes, w_first, w_second, cotangent):
    kernel_one, kernel_two = (
        lax.all_gather(w_first, "dp", axis=0, tiled=True),
        lax.all_gather(w_second, "dp", axis=0, tiled=True),
    )
    in_width = volumes.shape[1]
    mid_width = kernel_one.shape[1]
    count_one = lax.axis_size("dp") * lax.axis_size("space") * (volumes.size // in_width)
    factor_one = float(count_one) ** (-0.5)
    factor_two = float(count_one // 8) ** (-0.5)
    input_padded = with_halo(volumes, (("space", 2),), 1)
    first_pre = conv_forward(input_padded, kernel_one)
    first_pool = pooling(jax.nn.silu(first_pre)).astype(jnp.bfloat16)
    pool_padded = with_halo(first_pool, (("space", 2),), 1)
    second_pre = conv_forward(pool_padded, kernel_two)
    pooled = pooling(jax.nn.silu(second_pre)).astype(jnp.bfloat16)
    second_delta = (
        spread_up(cotangent.astype(jnp.float32)) * 0.125 * silu_slope(second_pre)
    ).astype(jnp.bfloat16)
    grad_two = conv_weight_grad(pool_padded, second_delta) * factor_two
    delta_padded = with_halo(second_delta, (("space", 2),), 1)
    pool_grad = conv_input_grad(delta_padded, kernel_two, mid_width).astype(jnp.bfloat16)
    first_delta = (spread_up(pool_grad.astype(jnp.float32)) * 0.125 * silu_slope(first_pre)).astype(
        jnp.bfloat16
    )
    grad_one = conv_weight_grad(input_padded, first_delta) * factor_one
    first_padded = with_halo(first_delta, (("space", 2),), 1)
    volume_grad = conv_input_grad(first_padded, kernel_one, in_width).astype(jnp.bfloat16)
    rows_one, rows_two = (
        lax.psum_scatter(
            grad_one.astype(jnp.bfloat16), "dp", scatter_dimension=0, tiled=True
        ).astype(jnp.float32),
        lax.psum_scatter(
            grad_two.astype(jnp.bfloat16), "dp", scatter_dimension=0, tiled=True
        ).astype(jnp.float32),
    )
    share_one, share_two = (
        lax.psum(rows_one.astype(jnp.bfloat16), "space").astype(jnp.float32),
        lax.psum(rows_two.astype(jnp.bfloat16), "space").astype(jnp.float32),
    )
    return (pooled, volume_grad, share_one, share_two)


def solution(mesh):
    return jax.shard_map(
        local,
        mesh=mesh,
        in_specs=(
            P("dp", None, "space", None, None),
            P("dp", None),
            P("dp", None),
            P("dp", None, "space", None, None),
        ),
        out_specs=(
            P("dp", None, "space", None, None),
            P("dp", None, "space", None, None),
            P("dp", None),
            P("dp", None),
        ),
        check_vma=False,
    )
```

profile of v0, /device:TPU:18, one launch (start us, length us, event | category | flops | bytes accessed | tf_op | source)
XLA Modules:
  0.0 181.7 jit_solution(16908317429202196970)
XLA Ops:
  0.6 1.1 copy.81
  1.7 1.3 collective-permute-start
  3.0 4.5 %collective-permute-start.1 = (bf16[1,32,1,8,128]{4,1,3,2,0:T(8,128)(2,1)S(1)}, bf16[1,32,1,8,128]{4,1,3,2,0:T(8,128)(2,1)S(1)}, u32[]{:S(2)}, u32[]{:S(2)}) collective-permute-start(bf16[1,32,1,8,128]{4,1,3,2,0:T(8,128)(2,1)S(1)} %get-tuple-element.27), channel_id=1, source_target_pairs={{1,0},{3,2},{5,4},{7,6},{9,8},{11,10},{13,12},{15,14},{17,16},{19,... | collective-permute-start | bytes 196616 | tf_op jit(solution)/shard_map/ppermute | solution.py:15
  7.6 0.7 multiply_bitcast_fusion
  8.3 16.8 %all-gather = bf16[16,54,64]{2,1,0:T(8,128)(2,1)S(1)} all-gather(bf16[1,54,64]{2,1,0:T(8,128)(2,1)} %bitcast.1526), channel_id=1, replica_groups=mesh['dp'=16,'space'=2] {'dp'}, dimensions={0}, use_global_device_ids=true | all-gather | bytes 117504 | tf_op jit(solution)/shard_map/all_gather | solution.py:120
  34.7 0.6 fusion.17
  35.7 1.9 %fusion.134 = (f32[64,4,8,128]{3,0,2,1:T(8,128)}, f32[64,4,8,128]{3,0,2,1:T(8,128)}) fusion(f32[64,4,8,128]{3,0,2,1:T(8,128)S(1)} %convolution_bitcast_fusion, f32[64,4,8,128]{3,0,2,1:T(8,128)S(1)} %convolution_bitcast_fusion.1, f32[64,4,8,128]{3,0,2,1:T(8,128)S(1)} %convolution_bitcast_fusion.2, f32[64,4,8,128]{3,0,2,1:T(8,128)S(1)} %convolution_bitcast_fusion.3, ...), kind=kOutput, calls=%fused_computation.293 | convolution fusion | flops 19267584 | bytes 7675904 | tf_op jit(solution)/shard_map/sixyz,io->soxyz/dot_general | solution.py:41
  37.6 1.8 %copy.87 = f32[64,4,8,128]{0,3,2,1:T(8,128)S(1)} copy(f32[64,4,8,128]{3,0,2,1:T(8,128)} %get-tuple-element.32) | data formatting | bytes 2097152 | tf_op jit(solution)/shard_map/jit(silu)/mul | solution.py:130
  39.5 2.4 %reduce_sum.21 = f32[64,2,4,64]{0,3,2,1:T(8,128)} reduce(f32[64,2,2,4,2,64,2]{0,6,5,4,3,2,1:T(2,128)S(1)} %bitcast.1517, f32[]{:T(128)} %constant.8.clone.1), dimensions={2,4,6}, to_apply=%region_0.1 | reduce | flops 229376 | bytes 1179652 | tf_op jit(solution)/shard_map/reduce_sum | solution.py:101
  41.9 1.0 fusion.210
  42.9 1.3 collective-permute-start.2
  44.2 4.5 %collective-permute-start.3 = (bf16[1,64,1,4,64]{1,4,3,2,0:T(8,128)(2,1)S(1)}, bf16[1,64,1,4,64]{1,4,3,2,0:T(8,128)(2,1)S(1)}, u32[]{:S(2)}, u32[]{:S(2)}) collective-permute-start(bf16[1,64,1,4,64]{1,4,3,2,0:T(8,128)(2,1)S(1)} %get-tuple-element.31), channel_id=1, source_target_pairs={{1,0},{3,2},{5,4},{7,6},{9,8},{11,10},{13,12},{15,14},{17,16},{19,... | collective-permute-start | bytes 98312 | tf_op jit(solution)/shard_map/ppermute | solution.py:15
  48.7 18.7 %all-gather.1 = bf16[16,108,128]{2,1,0:T(8,128)(2,1)S(1)} all-gather(bf16[1,108,128]{2,1,0:T(8,128)(2,1)S(1)} %bitcast.1525), channel_id=1, replica_groups=mesh['dp'=16,'space'=2] {'dp'}, dimensions={0}, use_global_device_ids=true | all-gather | bytes 470016 | tf_op jit(solution)/shard_map/all_gather | solution.py:121
  80.2 0.9 multiply_convert_fusion.1
  81.1 1.3 collective-permute-start.4
  82.4 4.5 %collective-permute-start.5 = (bf16[1,128,1,4,64]{1,4,3,2,0:T(8,128)(2,1)S(1)}, bf16[1,128,1,4,64]{1,4,3,2,0:T(8,128)(2,1)S(1)}, u32[]{:S(2)}, u32[]{:S(2)}) collective-permute-start(bf16[1,128,1,4,64]{1,4,3,2,0:T(8,128)(2,1)S(1)} %get-tuple-element.29), channel_id=1, source_target_pairs={{1,0},{3,2},{5,4},{7,6},{9,8},{11,10},{13,12},{15,14},{17,16},{19,... | collective-permute-start | bytes 196616 | tf_op jit(solution)/shard_map/ppermute | solution.py:15
  87.6 1.2 collective-permute-done.5
  93.8 0.9 broadcast_in_dim.16
  94.7 1.6 copy.88
  96.3 1.9 %multiply_convert_fusion = bf16[64,4,8,128]{3,0,2,1:T(8,128)(2,1)S(1)} fusion(f32[64,4,8,128]{3,0,2,1:T(8,128)} %copy.88, f32[64,4,8,128]{3,0,2,1:T(8,128)} %get-tuple-element.33), kind=kLoop, calls=%fused_computation.291 | loop fusion | flops 2359296 | bytes 2621440 | tf_op jit(solution)/shard_map/convert_element_type | solution.py:140
  106.5 30.5 %fusion.211 = (bf16[64,64]{1,0:T(8,128)(2,1)S(1)}, bf16[112,128]{1,0:T(8,128)(2,1)S(1)}) fusion(bf16[864,64]{1,0:T(8,128)(2,1)S(1)} %bitcast.1522, bf16[1728,128]{1,0:T(8,128)(2,1)S(1)} %bitcast.1521), kind=kCustom, calls=%all-reduce-scatter.2 | all-reduce-scatter fusion | flops 294914 | bytes 590336
  137.0 1.9 %collective-permute-start.8 = (bf16[64,64]{1,0:T(8,128)(2,1)S(1)}, bf16[64,64]{1,0:T(8,128)(2,1)S(1)}, u32[]{:S(2)}, u32[]{:S(2)}) collective-permute-start(bf16[64,64]{1,0:T(8,128)(2,1)S(1)} %get-tuple-element.20), channel_id=1, source_target_pairs={{0,2},{2,4},{4,6},{6,8},{8,10},{10,12},{12,14},{14,16},{16,18},{18... | collective-permute-start | bytes 24584
  138.9 1.9 %collective-permute-start.9 = (bf16[64,64]{1,0:T(8,128)(2,1)S(1)}, bf16[64,64]{1,0:T(8,128)(2,1)S(1)}, u32[]{:S(2)}, u32[]{:S(2)}) collective-permute-start(bf16[64,64]{1,0:T(8,128)(2,1)S(1)} %get-tuple-element.20), channel_id=1, source_target_pairs={{0,4},{2,6},{4,8},{6,10},{8,12},{10,14},{12,16},{14,18},{16,20},{1... | collective-permute-start | bytes 24584
  141.1 4.0 %collective-permute-start.11 = (bf16[60,128]{1,0:T(8,128)(2,1)S(1)}, bf16[60,128]{1,0:T(8,128)(2,1)S(1)}, u32[]{:S(2)}, u32[]{:S(2)}) collective-permute-start(bf16[60,128]{1,0:T(8,128)(2,1)S(1)} %slice.955), channel_id=1, source_target_pairs={{0,2},{2,4},{4,6},{6,8},{8,10},{10,12},{12,14},{14,16},{16,18},{18... | collective-permute-start | bytes 46088
  145.1 9.2 %collective-permute-start.10 = (bf16[22,64]{1,0:T(8,128)(2,1)S(1)}, bf16[22,64]{1,0:T(8,128)(2,1)S(1)}, u32[]{:S(2)}, u32[]{:S(2)}) collective-permute-start(bf16[22,64]{1,0:T(8,128)(2,1)S(1)} %slice.954), channel_id=1, source_target_pairs={{0,6},{2,8},{4,10},{6,12},{8,14},{10,16},{12,18},{14,20},{16,22},{... | collective-permute-start | bytes 8456
  154.3 3.9 %collective-permute-start.7 = (bf16[1,64,1,8,128]{4,1,3,2,0:T(8,128)(2,1)S(1)}, bf16[1,64,1,8,128]{4,1,3,2,0:T(8,128)(2,1)S(1)}, u32[]{:S(2)}, u32[]{:S(2)}) collective-permute-start(bf16[1,64,1,8,128]{4,1,3,2,0:T(8,128)(2,1)S(1)} %get-tuple-element.23), channel_id=1, source_target_pairs={{1,0},{3,2},{5,4},{7,6},{9,8},{11,10},{13,12},{15,14},{17,16},{19,... | collective-permute-start | bytes 393224 | tf_op jit(solution)/shard_map/ppermute | solution.py:15
  158.3 1.3 collective-permute-start.6
  160.5 9.7 %all-reduce.8 = (bf16[54,64]{1,0:T(8,128)(2,1)S(1)}, bf16[108,128]{1,0:T(8,128)(2,1)S(1)}) all-reduce(bf16[54,64]{1,0:T(8,128)(2,1)S(1)} %constant_dynamic-slice_fusion.1, bf16[108,128]{1,0:T(8,128)(2,1)S(1)} %constant_dynamic-slice_fusion), channel_id=1, replica_groups=mesh['dp'=16,'space'=2] {'space'}, use_global_device_ids=true, to_apply=%region_4.5 | all-reduce | flops 17280 | bytes 69120 | tf_op jit(solution)/shard_map/psum | solution.py:155
  170.3 0.6 convert_element_type.112
  171.5 1.1 select_maximum_fusion
  179.4 0.7 fusion.50
  180.9 0.8 copy.117
  (207 shorter events, 43.8 us)
Async XLA Ops:
  1.7 23.5 %collective-permute-start = (bf16[1,32,1,8,128]{4,1,3,2,0:T(8,128)(2,1)S(1)}, bf16[1,32,1,8,128]{4,1,3,2,0:T(8,128)(2,1)S(1)}, u32[]{:S(2)}, u32[]{:S(2)}) collective-permute-start(bf16[1,32,1,8,128]{4,1,3,2,0:T(8,128)(2,1)S(1)} %get-tuple-element.26), channel_id=1, source_target_pairs={{0,1},{2,3},{4,5},{6,7},{8,9},{10,11},{12,13},{14,15},{16,17},{18,... | collective-permute-start | bytes 196616 | tf_op jit(solution)/shard_map/ppermute | solution.py:12
  3.0 22.2 %collective-permute-start.1 = (bf16[1,32,1,8,128]{4,1,3,2,0:T(8,128)(2,1)S(1)}, bf16[1,32,1,8,128]{4,1,3,2,0:T(8,128)(2,1)S(1)}, u32[]{:S(2)}, u32[]{:S(2)}) collective-permute-start(bf16[1,32,1,8,128]{4,1,3,2,0:T(8,128)(2,1)S(1)} %get-tuple-element.27), channel_id=1, source_target_pairs={{1,0},{3,2},{5,4},{7,6},{9,8},{11,10},{13,12},{15,14},{17,16},{19,... | collective-permute-start | bytes 196616 | tf_op jit(solution)/shard_map/ppermute | solution.py:15
  25.2 10.5 %copy-start.3 = (bf16[3,3,3,32,64]{4,3,2,1,0:T(8,128)(2,1)}, bf16[3,3,3,32,64]{4,3,2,1,0:T(8,128)(2,1)S(1)}, u32[]{:S(2)}) copy-start(bf16[3,3,3,32,64]{4,3,2,1,0:T(8,128)(2,1)S(1)} %reshape.915) | copy-start | bytes 331780
  33.4 1.0 copy-start.1
  39.4 9.3 %copy-start.6 = (bf16[108,128]{1,0:T(8,128)(2,1)S(1)}, bf16[108,128]{1,0:T(8,128)(2,1)}, u32[]{:S(2)}) copy-start(bf16[108,128]{1,0:T(8,128)(2,1)} %param.6) | copy-start | bytes 82948
  39.4 28.1 %copy-start.7 = (u32[32]{0:T(128)S(1)}, u32[32]{0:T(128)}, u32[]{:S(2)}) copy-start(u32[32]{0:T(128)} %constant.37) | copy-start | bytes 388
  42.9 26.6 %collective-permute-start.2 = (bf16[1,64,1,4,64]{1,4,3,2,0:T(8,128)(2,1)S(1)}, bf16[1,64,1,4,64]{1,4,3,2,0:T(8,128)(2,1)S(1)}, u32[]{:S(2)}, u32[]{:S(2)}) collective-permute-start(bf16[1,64,1,4,64]{1,4,3,2,0:T(8,128)(2,1)S(1)} %get-tuple-element.30), channel_id=1, source_target_pairs={{0,1},{2,3},{4,5},{6,7},{8,9},{10,11},{12,13},{14,15},{16,17},{18,... | collective-permute-start | bytes 98312 | tf_op jit(solution)/shard_map/ppermute | solution.py:12
  44.2 25.3 %collective-permute-start.3 = (bf16[1,64,1,4,64]{1,4,3,2,0:T(8,128)(2,1)S(1)}, bf16[1,64,1,4,64]{1,4,3,2,0:T(8,128)(2,1)S(1)}, u32[]{:S(2)}, u32[]{:S(2)}) collective-permute-start(bf16[1,64,1,4,64]{1,4,3,2,0:T(8,128)(2,1)S(1)} %get-tuple-element.31), channel_id=1, source_target_pairs={{1,0},{3,2},{5,4},{7,6},{9,8},{11,10},{13,12},{15,14},{17,16},{19,... | collective-permute-start | bytes 98312 | tf_op jit(solution)/shard_map/ppermute | solution.py:15
  71.3 1.0 copy-start
  81.1 6.6 %collective-permute-start.4 = (bf16[1,128,1,4,64]{1,4,3,2,0:T(8,128)(2,1)S(1)}, bf16[1,128,1,4,64]{1,4,3,2,0:T(8,128)(2,1)S(1)}, u32[]{:S(2)}, u32[]{:S(2)}) collective-permute-start(bf16[1,128,1,4,64]{1,4,3,2,0:T(8,128)(2,1)S(1)} %get-tuple-element.28), channel_id=1, source_target_pairs={{0,1},{2,3},{4,5},{6,7},{8,9},{10,11},{12,13},{14,15},{16,17},{18,... | collective-permute-start | bytes 196616 | tf_op jit(solution)/shard_map/ppermute | solution.py:12
  82.4 6.4 %collective-permute-start.5 = (bf16[1,128,1,4,64]{1,4,3,2,0:T(8,128)(2,1)S(1)}, bf16[1,128,1,4,64]{1,4,3,2,0:T(8,128)(2,1)S(1)}, u32[]{:S(2)}, u32[]{:S(2)}) collective-permute-start(bf16[1,128,1,4,64]{1,4,3,2,0:T(8,128)(2,1)S(1)} %get-tuple-element.29), channel_id=1, source_target_pairs={{1,0},{3,2},{5,4},{7,6},{9,8},{11,10},{13,12},{15,14},{17,16},{19,... | collective-permute-start | bytes 196616 | tf_op jit(solution)/shard_map/ppermute | solution.py:15
  100.6 1.5 copy-start.2
  105.2 1.3 copy-start.5
  105.5 35.4 %copy-start.4 = (bf16[3,3,3,32,64]{4,3,2,1,0:T(8,128)(2,1)S(1)}, bf16[3,3,3,32,64]{4,3,2,1,0:T(8,128)(2,1)}, u32[]{:S(2)}) copy-start(bf16[3,3,3,32,64]{4,3,2,1,0:T(8,128)(2,1)} %copy-done.3) | copy-start | bytes 331780
  137.0 22.6 %collective-permute-start.8 = (bf16[64,64]{1,0:T(8,128)(2,1)S(1)}, bf16[64,64]{1,0:T(8,128)(2,1)S(1)}, u32[]{:S(2)}, u32[]{:S(2)}) collective-permute-start(bf16[64,64]{1,0:T(8,128)(2,1)S(1)} %get-tuple-element.20), channel_id=1, source_target_pairs={{0,2},{2,4},{4,6},{6,8},{8,10},{10,12},{12,14},{14,16},{16,18},{18... | collective-permute-start | bytes 24584
  138.9 20.6 %collective-permute-start.9 = (bf16[64,64]{1,0:T(8,128)(2,1)S(1)}, bf16[64,64]{1,0:T(8,128)(2,1)S(1)}, u32[]{:S(2)}, u32[]{:S(2)}) collective-permute-start(bf16[64,64]{1,0:T(8,128)(2,1)S(1)} %get-tuple-element.20), channel_id=1, source_target_pairs={{0,4},{2,6},{4,8},{6,10},{8,12},{10,14},{12,16},{14,18},{16,20},{1... | collective-permute-start | bytes 24584
  141.1 19.1 %collective-permute-start.11 = (bf16[60,128]{1,0:T(8,128)(2,1)S(1)}, bf16[60,128]{1,0:T(8,128)(2,1)S(1)}, u32[]{:S(2)}, u32[]{:S(2)}) collective-permute-start(bf16[60,128]{1,0:T(8,128)(2,1)S(1)} %slice.955), channel_id=1, source_target_pairs={{0,2},{2,4},{4,6},{6,8},{8,10},{10,12},{12,14},{14,16},{16,18},{18... | collective-permute-start | bytes 46088
  145.1 13.1 %collective-permute-start.10 = (bf16[22,64]{1,0:T(8,128)(2,1)S(1)}, bf16[22,64]{1,0:T(8,128)(2,1)S(1)}, u32[]{:S(2)}, u32[]{:S(2)}) collective-permute-start(bf16[22,64]{1,0:T(8,128)(2,1)S(1)} %slice.954), channel_id=1, source_target_pairs={{0,6},{2,8},{4,10},{6,12},{8,14},{10,16},{12,18},{14,20},{16,22},{... | collective-permute-start | bytes 8456
  154.3 17.2 %collective-permute-start.7 = (bf16[1,64,1,8,128]{4,1,3,2,0:T(8,128)(2,1)S(1)}, bf16[1,64,1,8,128]{4,1,3,2,0:T(8,128)(2,1)S(1)}, u32[]{:S(2)}, u32[]{:S(2)}) collective-permute-start(bf16[1,64,1,8,128]{4,1,3,2,0:T(8,128)(2,1)S(1)} %get-tuple-element.23), channel_id=1, source_target_pairs={{1,0},{3,2},{5,4},{7,6},{9,8},{11,10},{13,12},{15,14},{17,16},{19,... | collective-permute-start | bytes 393224 | tf_op jit(solution)/shard_map/ppermute | solution.py:15
  158.3 13.2 %collective-permute-start.6 = (bf16[1,64,1,8,128]{4,1,3,2,0:T(8,128)(2,1)S(1)}, bf16[1,64,1,8,128]{4,1,3,2,0:T(8,128)(2,1)S(1)}, u32[]{:S(2)}, u32[]{:S(2)}) collective-permute-start(bf16[1,64,1,8,128]{4,1,3,2,0:T(8,128)(2,1)S(1)} %get-tuple-element.22), channel_id=1, source_target_pairs={{0,1},{2,3},{4,5},{6,7},{8,9},{10,11},{12,13},{14,15},{16,17},{18,... | collective-permute-start | bytes 393224 | tf_op jit(solution)/shard_map/ppermute | solution.py:12
where the time goes:
time: 182 us
  blocking collectives  75.8 us (42%)
  matrix products  43 us (24%)
  starting transfers between devices  39.7 us (22%)
  other arithmetic  10.6 us (6%)
  local copies, waits for them, and re-layouts  8.21 us (5%)
  between operations  3.1 us (2%)
    unnamed x1, blocking collectives  30.5 us
    all_gather x1, blocking collectives, local(): lax.all_gather(w_second, 'dp', axis=0, tiled=True)  18.7 us
    ppermute x4, starting transfers between devices, with_halo(): lax.ppermute(lax.slice_in_dim(block, 0, width, axis=dim), axis, backward)  17.6 us
    unnamed x4, starting transfers between devices  17 us
    all_gather x1, blocking collectives, local(): lax.all_gather(w_first, 'dp', axis=0, tiled=True)  16.8 us
    dot_general x54, matrix products, conv_forward(): jnp.einsum('sixyz,io->soxyz', window, kernel[along_x, along_y, along_z],...  16.1 us
    dot_general x54, matrix products, conv_weight_grad(): jnp.einsum('sixyz,soxyz->io', window, grads, preferred_element_type=jnp.f...  13.8 us
    dot_general x54, matrix products, conv_input_grad(): jnp.einsum('soxyz,io->sixyz', window, kernel[along_x, along_y, along_z],...  13.1 us
  transfers between devices with their start and end apart: 12, of which 1 were waited for; matrix products, arithmetic and copies ran while one was open for 2% of the time, Pallas kernels for 0%

commit v1 on v0

--- a/solution.py
+++ b/solution.py
@@ -152,7 +152,7 @@
         ).astype(jnp.float32),
     )
     share_one, share_two = (
-        lax.psum(rows_one.astype(jnp.bfloat16), "space").astype(jnp.float32),
+        jnp.sum(lax.all_gather(rows_one.astype(jnp.bfloat16), "space"), axis=0).astype(jnp.float32),
         lax.psum(rows_two.astype(jnp.bfloat16), "space").astype(jnp.float32),
     )
     return (pooled, volume_grad, share_one, share_two)

time: 182 us -> 187 us (1.027)
  blocking collectives: 75.8 us -> 80 us
    all_gather x0 -> x1, blocking collectives: none -> 5.12 us  [local(): lax.all_gather(rows_one.astype(jnp.bfloat16), 'space')]
where the time goes in v1:
time: 187 us; the launch traced here: 186 us
  blocking collectives  80 us (43%)
  matrix products  43 us (23%)
  starting transfers between devices  39.7 us (21%)
  other arithmetic  10.6 us (6%)
  local copies, waits for them, and re-layouts  8.23 us (4%)
  between operations  3.09 us (2%)
    unnamed x1, blocking collectives  30.5 us
    all_gather x1, blocking collectives, local(): lax.all_gather(w_second, 'dp', axis=0, tiled=True)  18.7 us
    ppermute x4, starting transfers between devices, with_halo(): lax.ppermute(lax.slice_in_dim(block, 0, width, axis=dim), axis, backward)  17.6 us
    unnamed x4, starting transfers between devices  17 us
    all_gather x1, blocking collectives, local(): lax.all_gather(w_first, 'dp', axis=0, tiled=True)  16.8 us
    dot_general x54, matrix products, conv_forward(): jnp.einsum('sixyz,io->soxyz', window, kernel[along_x, along_y, along_z],...  16.1 us
    dot_general x54, matrix products, conv_weight_grad(): jnp.einsum('sixyz,soxyz->io', window, grads, preferred_element_type=jnp.f...  13.8 us
    dot_general x54, matrix products, conv_input_grad(): jnp.einsum('soxyz,io->sixyz', window, kernel[along_x, along_y, along_z],...  13.1 us
  transfers between devices with their start and end apart: 12, of which 1 were waited for; matrix products, arithmetic and copies ran while one was open for 2% of the time, Pallas kernels for 0%

profile of v1, /device:TPU:18, one launch (start us, length us, event | category | flops | bytes accessed | tf_op | source)
XLA Modules:
  0.0 185.9 jit_solution(1503995329860898905)
XLA Ops:
  0.6 1.1 copy.81
  1.7 1.3 collective-permute-start
  3.0 4.5 %collective-permute-start.1 = (bf16[1,32,1,8,128]{4,1,3,2,0:T(8,128)(2,1)S(1)}, bf16[1,32,1,8,128]{4,1,3,2,0:T(8,128)(2,1)S(1)}, u32[]{:S(2)}, u32[]{:S(2)}) collective-permute-start(bf16[1,32,1,8,128]{4,1,3,2,0:T(8,128)(2,1)S(1)} %get-tuple-element.25), channel_id=1, source_target_pairs={{1,0},{3,2},{5,4},{7,6},{9,8},{11,10},{13,12},{15,14},{17,16},{19,... | collective-permute-start | bytes 196616 | tf_op jit(solution)/shard_map/ppermute | solution.py:15
  7.6 0.7 multiply_bitcast_fusion
  8.3 16.8 %all-gather.1 = bf16[16,54,64]{2,1,0:T(8,128)(2,1)S(1)} all-gather(bf16[1,54,64]{2,1,0:T(8,128)(2,1)} %bitcast.1528), channel_id=1, replica_groups=mesh['dp'=16,'space'=2] {'dp'}, dimensions={0}, use_global_device_ids=true | all-gather | bytes 117504 | tf_op jit(solution)/shard_map/all_gather | solution.py:120
  34.7 0.6 fusion.17
  35.7 2.0 %fusion.134 = (f32[64,4,8,128]{3,0,2,1:T(8,128)}, f32[64,4,8,128]{3,0,2,1:T(8,128)}) fusion(f32[64,4,8,128]{3,0,2,1:T(8,128)S(1)} %convolution_bitcast_fusion, f32[64,4,8,128]{3,0,2,1:T(8,128)S(1)} %convolution_bitcast_fusion.1, f32[64,4,8,128]{3,0,2,1:T(8,128)S(1)} %convolution_bitcast_fusion.2, f32[64,4,8,128]{3,0,2,1:T(8,128)S(1)} %convolution_bitcast_fusion.3, ...), kind=kOutput, calls=%fused_computation.293 | convolution fusion | flops 19267584 | bytes 7675904 | tf_op jit(solution)/shard_map/sixyz,io->soxyz/dot_general | solution.py:41
  37.6 1.8 copy.87
  39.5 2.4 %reduce_sum.37 = f32[64,2,4,64]{0,3,2,1:T(8,128)} reduce(f32[64,2,2,4,2,64,2]{0,6,5,4,3,2,1:T(2,128)S(1)} %bitcast.1519, f32[]{:T(128)} %constant.8.clone.1), dimensions={2,4,6}, to_apply=%region_0.1 | reduce | flops 229376 | bytes 1179652 | tf_op jit(solution)/shard_map/reduce_sum | solution.py:101
  41.9 1.0 fusion.210
  42.9 1.3 collective-permute-start.2
  44.2 4.5 %collective-permute-start.3 = (bf16[1,64,1,4,64]{1,4,3,2,0:T(8,128)(2,1)S(1)}, bf16[1,64,1,4,64]{1,4,3,2,0:T(8,128)(2,1)S(1)}, u32[]{:S(2)}, u32[]{:S(2)}) collective-permute-start(bf16[1,64,1,4,64]{1,4,3,2,0:T(8,128)(2,1)S(1)} %get-tuple-element.29), channel_id=1, source_target_pairs={{1,0},{3,2},{5,4},{7,6},{9,8},{11,10},{13,12},{15,14},{17,16},{19,... | collective-permute-start | bytes 98312 | tf_op jit(solution)/shard_map/ppermute | solution.py:15
  48.8 18.7 %all-gather.2 = bf16[16,108,128]{2,1,0:T(8,128)(2,1)S(1)} all-gather(bf16[1,108,128]{2,1,0:T(8,128)(2,1)S(1)} %bitcast.1527), channel_id=1, replica_groups=mesh['dp'=16,'space'=2] {'dp'}, dimensions={0}, use_global_device_ids=true | all-gather | bytes 470016 | tf_op jit(solution)/shard_map/all_gather | solution.py:121
  80.2 0.9 multiply_convert_fusion.1
  81.1 1.3 collective-permute-start.4
  82.4 4.5 %collective-permute-start.5 = (bf16[1,128,1,4,64]{1,4,3,2,0:T(8,128)(2,1)S(1)}, bf16[1,128,1,4,64]{1,4,3,2,0:T(8,128)(2,1)S(1)}, u32[]{:S(2)}, u32[]{:S(2)}) collective-permute-start(bf16[1,128,1,4,64]{1,4,3,2,0:T(8,128)(2,1)S(1)} %get-tuple-element.27), channel_id=1, source_target_pairs={{1,0},{3,2},{5,4},{7,6},{9,8},{11,10},{13,12},{15,14},{17,16},{19,... | collective-permute-start | bytes 196616 | tf_op jit(solution)/shard_map/ppermute | solution.py:15
  87.6 1.2 collective-permute-done.5
  93.8 0.9 broadcast_in_dim.16
  94.7 1.6 copy.88
  96.3 1.9 %multiply_convert_fusion = bf16[64,4,8,128]{3,0,2,1:T(8,128)(2,1)S(1)} fusion(f32[64,4,8,128]{3,0,2,1:T(8,128)} %copy.88, f32[64,4,8,128]{3,0,2,1:T(8,128)} %get-tuple-element.31), kind=kLoop, calls=%fused_computation.291 | loop fusion | flops 2359296 | bytes 2621440 | tf_op jit(solution)/shard_map/convert_element_type | solution.py:140
  106.5 30.5 %fusion.211 = (bf16[64,64]{1,0:T(8,128)(2,1)S(1)}, bf16[112,128]{1,0:T(8,128)(2,1)S(1)}) fusion(bf16[864,64]{1,0:T(8,128)(2,1)S(1)} %bitcast.1524, bf16[1728,128]{1,0:T(8,128)(2,1)S(1)} %bitcast.1523), kind=kCustom, calls=%all-reduce-scatter.2 | all-reduce-scatter fusion | flops 294914 | bytes 590336
  137.0 1.9 %collective-permute-start.8 = (bf16[64,64]{1,0:T(8,128)(2,1)S(1)}, bf16[64,64]{1,0:T(8,128)(2,1)S(1)}, u32[]{:S(2)}, u32[]{:S(2)}) collective-permute-start(bf16[64,64]{1,0:T(8,128)(2,1)S(1)} %get-tuple-element.18), channel_id=1, source_target_pairs={{0,2},{2,4},{4,6},{6,8},{8,10},{10,12},{12,14},{14,16},{16,18},{18... | collective-permute-start | bytes 24584
  139.0 1.9 %collective-permute-start.9 = (bf16[64,64]{1,0:T(8,128)(2,1)S(1)}, bf16[64,64]{1,0:T(8,128)(2,1)S(1)}, u32[]{:S(2)}, u32[]{:S(2)}) collective-permute-start(bf16[64,64]{1,0:T(8,128)(2,1)S(1)} %get-tuple-element.18), channel_id=1, source_target_pairs={{0,4},{2,6},{4,8},{6,10},{8,12},{10,14},{12,16},{14,18},{16,20},{1... | collective-permute-start | bytes 24584
  141.1 4.0 %collective-permute-start.11 = (bf16[60,128]{1,0:T(8,128)(2,1)S(1)}, bf16[60,128]{1,0:T(8,128)(2,1)S(1)}, u32[]{:S(2)}, u32[]{:S(2)}) collective-permute-start(bf16[60,128]{1,0:T(8,128)(2,1)S(1)} %slice.955), channel_id=1, source_target_pairs={{0,2},{2,4},{4,6},{6,8},{8,10},{10,12},{12,14},{14,16},{16,18},{18... | collective-permute-start | bytes 46088
  145.1 9.2 %collective-permute-start.10 = (bf16[22,64]{1,0:T(8,128)(2,1)S(1)}, bf16[22,64]{1,0:T(8,128)(2,1)S(1)}, u32[]{:S(2)}, u32[]{:S(2)}) collective-permute-start(bf16[22,64]{1,0:T(8,128)(2,1)S(1)} %slice.954), channel_id=1, source_target_pairs={{0,6},{2,8},{4,10},{6,12},{8,14},{10,16},{12,18},{14,20},{16,22},{... | collective-permute-start | bytes 8456
  154.4 3.9 %collective-permute-start.7 = (bf16[1,64,1,8,128]{4,1,3,2,0:T(8,128)(2,1)S(1)}, bf16[1,64,1,8,128]{4,1,3,2,0:T(8,128)(2,1)S(1)}, u32[]{:S(2)}, u32[]{:S(2)}) collective-permute-start(bf16[1,64,1,8,128]{4,1,3,2,0:T(8,128)(2,1)S(1)} %get-tuple-element.21), channel_id=1, source_target_pairs={{1,0},{3,2},{5,4},{7,6},{9,8},{11,10},{13,12},{15,14},{17,16},{19,... | collective-permute-start | bytes 393224 | tf_op jit(solution)/shard_map/ppermute | solution.py:15
  158.3 1.3 collective-permute-start.6
  160.2 5.1 %all-gather.3 = bf16[2,54,64]{2,1,0:T(8,128)(2,1)S(1)} all-gather(bf16[1,54,64]{2,1,0:T(8,128)(2,1)S(1)} %dynamic-slice_bitcast_fusion), channel_id=2, replica_groups=mesh['dp'=16,'space'=2] {'space'}, dimensions={0}, use_global_device_ids=true | all-gather | bytes 20736 | tf_op jit(solution)/shard_map/all_gather | solution.py:155
  166.3 8.8 %psum.7 = bf16[108,128]{1,0:T(8,128)(2,1)S(1)} all-reduce(bf16[108,128]{1,0:T(8,128)(2,1)S(1)} %constant_dynamic-slice_fusion), channel_id=1, replica_groups=mesh['dp'=16,'space'=2] {'space'}, use_global_device_ids=true, to_apply=%region_6.7 | all-reduce | flops 13824 | bytes 55296 | tf_op jit(solution)/shard_map/psum | solution.py:156
  175.7 1.1 select_maximum_fusion
  183.5 0.7 fusion.50
  185.1 0.8 copy.117
  (209 shorter events, 44.4 us)
Async XLA Ops:
  1.7 23.5 %collective-permute-start = (bf16[1,32,1,8,128]{4,1,3,2,0:T(8,128)(2,1)S(1)}, bf16[1,32,1,8,128]{4,1,3,2,0:T(8,128)(2,1)S(1)}, u32[]{:S(2)}, u32[]{:S(2)}) collective-permute-start(bf16[1,32,1,8,128]{4,1,3,2,0:T(8,128)(2,1)S(1)} %get-tuple-element.24), channel_id=1, source_target_pairs={{0,1},{2,3},{4,5},{6,7},{8,9},{10,11},{12,13},{14,15},{16,17},{18,... | collective-permute-start | bytes 196616 | tf_op jit(solution)/shard_map/ppermute | solution.py:12
  3.0 22.2 %collective-permute-start.1 = (bf16[1,32,1,8,128]{4,1,3,2,0:T(8,128)(2,1)S(1)}, bf16[1,32,1,8,128]{4,1,3,2,0:T(8,128)(2,1)S(1)}, u32[]{:S(2)}, u32[]{:S(2)}) collective-permute-start(bf16[1,32,1,8,128]{4,1,3,2,0:T(8,128)(2,1)S(1)} %get-tuple-element.25), channel_id=1, source_target_pairs={{1,0},{3,2},{5,4},{7,6},{9,8},{11,10},{13,12},{15,14},{17,16},{19,... | collective-permute-start | bytes 196616 | tf_op jit(solution)/shard_map/ppermute | solution.py:15
  25.2 10.5 %copy-start.3 = (bf16[3,3,3,32,64]{4,3,2,1,0:T(8,128)(2,1)}, bf16[3,3,3,32,64]{4,3,2,1,0:T(8,128)(2,1)S(1)}, u32[]{:S(2)}) copy-start(bf16[3,3,3,32,64]{4,3,2,1,0:T(8,128)(2,1)S(1)} %reshape.915) | copy-start | bytes 331780
  33.4 1.0 copy-start.1
  39.5 9.3 %copy-start.6 = (bf16[108,128]{1,0:T(8,128)(2,1)S(1)}, bf16[108,128]{1,0:T(8,128)(2,1)}, u32[]{:S(2)}) copy-start(bf16[108,128]{1,0:T(8,128)(2,1)} %param.6) | copy-start | bytes 82948
  39.5 28.1 %copy-start.7 = (u32[32]{0:T(128)S(1)}, u32[32]{0:T(128)}, u32[]{:S(2)}) copy-start(u32[32]{0:T(128)} %constant.38) | copy-start | bytes 388
  42.9 26.6 %collective-permute-start.2 = (bf16[1,64,1,4,64]{1,4,3,2,0:T(8,128)(2,1)S(1)}, bf16[1,64,1,4,64]{1,4,3,2,0:T(8,128)(2,1)S(1)}, u32[]{:S(2)}, u32[]{:S(2)}) collective-permute-start(bf16[1,64,1,4,64]{1,4,3,2,0:T(8,128)(2,1)S(1)} %get-tuple-element.28), channel_id=1, source_target_pairs={{0,1},{2,3},{4,5},{6,7},{8,9},{10,11},{12,13},{14,15},{16,17},{18,... | collective-permute-start | bytes 98312 | tf_op jit(solution)/shard_map/ppermute | solution.py:12
  44.2 25.3 %collective-permute-start.3 = (bf16[1,64,1,4,64]{1,4,3,2,0:T(8,128)(2,1)S(1)}, bf16[1,64,1,4,64]{1,4,3,2,0:T(8,128)(2,1)S(1)}, u32[]{:S(2)}, u32[]{:S(2)}) collective-permute-start(bf16[1,64,1,4,64]{1,4,3,2,0:T(8,128)(2,1)S(1)} %get-tuple-element.29), channel_id=1, source_target_pairs={{1,0},{3,2},{5,4},{7,6},{9,8},{11,10},{13,12},{15,14},{17,16},{19,... | collective-permute-start | bytes 98312 | tf_op jit(solution)/shard_map/ppermute | solution.py:15
  71.3 1.0 copy-start
  81.1 6.6 %collective-permute-start.4 = (bf16[1,128,1,4,64]{1,4,3,2,0:T(8,128)(2,1)S(1)}, bf16[1,128,1,4,64]{1,4,3,2,0:T(8,128)(2,1)S(1)}, u32[]{:S(2)}, u32[]{:S(2)}) collective-permute-start(bf16[1,128,1,4,64]{1,4,3,2,0:T(8,128)(2,1)S(1)} %get-tuple-element.26), channel_id=1, source_target_pairs={{0,1},{2,3},{4,5},{6,7},{8,9},{10,11},{12,13},{14,15},{16,17},{18,... | collective-permute-start | bytes 196616 | tf_op jit(solution)/shard_map/ppermute | solution.py:12
  82.4 6.4 %collective-permute-start.5 = (bf16[1,128,1,4,64]{1,4,3,2,0:T(8,128)(2,1)S(1)}, bf16[1,128,1,4,64]{1,4,3,2,0:T(8,128)(2,1)S(1)}, u32[]{:S(2)}, u32[]{:S(2)}) collective-permute-start(bf16[1,128,1,4,64]{1,4,3,2,0:T(8,128)(2,1)S(1)} %get-tuple-element.27), channel_id=1, source_target_pairs={{1,0},{3,2},{5,4},{7,6},{9,8},{11,10},{13,12},{15,14},{17,16},{19,... | collective-permute-start | bytes 196616 | tf_op jit(solution)/shard_map/ppermute | solution.py:15
  100.6 1.5 copy-start.2
  105.2 1.3 copy-start.5
  105.5 35.4 %copy-start.4 = (bf16[3,3,3,32,64]{4,3,2,1,0:T(8,128)(2,1)S(1)}, bf16[3,3,3,32,64]{4,3,2,1,0:T(8,128)(2,1)}, u32[]{:S(2)}) copy-start(bf16[3,3,3,32,64]{4,3,2,1,0:T(8,128)(2,1)} %copy-done.3) | copy-start | bytes 331780
  137.0 22.6 %collective-permute-start.8 = (bf16[64,64]{1,0:T(8,128)(2,1)S(1)}, bf16[64,64]{1,0:T(8,128)(2,1)S(1)}, u32[]{:S(2)}, u32[]{:S(2)}) collective-permute-start(bf16[64,64]{1,0:T(8,128)(2,1)S(1)} %get-tuple-element.18), channel_id=1, source_target_pairs={{0,2},{2,4},{4,6},{6,8},{8,10},{10,12},{12,14},{14,16},{16,18},{18... | collective-permute-start | bytes 24584
  139.0 20.6 %collective-permute-start.9 = (bf16[64,64]{1,0:T(8,128)(2,1)S(1)}, bf16[64,64]{1,0:T(8,128)(2,1)S(1)}, u32[]{:S(2)}, u32[]{:S(2)}) collective-permute-start(bf16[64,64]{1,0:T(8,128)(2,1)S(1)} %get-tuple-element.18), channel_id=1, source_target_pairs={{0,4},{2,6},{4,8},{6,10},{8,12},{10,14},{12,16},{14,18},{16,20},{1... | collective-permute-start | bytes 24584
  141.1 24.8 %collective-permute-start.11 = (bf16[60,128]{1,0:T(8,128)(2,1)S(1)}, bf16[60,128]{1,0:T(8,128)(2,1)S(1)}, u32[]{:S(2)}, u32[]{:S(2)}) collective-permute-start(bf16[60,128]{1,0:T(8,128)(2,1)S(1)} %slice.955), channel_id=1, source_target_pairs={{0,2},{2,4},{4,6},{6,8},{8,10},{10,12},{12,14},{14,16},{16,18},{18... | collective-permute-start | bytes 46088
  145.1 13.1 %collective-permute-start.10 = (bf16[22,64]{1,0:T(8,128)(2,1)S(1)}, bf16[22,64]{1,0:T(8,128)(2,1)S(1)}, u32[]{:S(2)}, u32[]{:S(2)}) collective-permute-start(bf16[22,64]{1,0:T(8,128)(2,1)S(1)} %slice.954), channel_id=1, source_target_pairs={{0,6},{2,8},{4,10},{6,12},{8,14},{10,16},{12,18},{14,20},{16,22},{... | collective-permute-start | bytes 8456
  154.4 21.3 %collective-permute-start.7 = (bf16[1,64,1,8,128]{4,1,3,2,0:T(8,128)(2,1)S(1)}, bf16[1,64,1,8,128]{4,1,3,2,0:T(8,128)(2,1)S(1)}, u32[]{:S(2)}, u32[]{:S(2)}) collective-permute-start(bf16[1,64,1,8,128]{4,1,3,2,0:T(8,128)(2,1)S(1)} %get-tuple-element.21), channel_id=1, source_target_pairs={{1,0},{3,2},{5,4},{7,6},{9,8},{11,10},{13,12},{15,14},{17,16},{19,... | collective-permute-start | bytes 393224 | tf_op jit(solution)/shard_map/ppermute | solution.py:15
  158.3 17.4 %collective-permute-start.6 = (bf16[1,64,1,8,128]{4,1,3,2,0:T(8,128)(2,1)S(1)}, bf16[1,64,1,8,128]{4,1,3,2,0:T(8,128)(2,1)S(1)}, u32[]{:S(2)}, u32[]{:S(2)}) collective-permute-start(bf16[1,64,1,8,128]{4,1,3,2,0:T(8,128)(2,1)S(1)} %get-tuple-element.20), channel_id=1, source_target_pairs={{0,1},{2,3},{4,5},{6,7},{8,9},{10,11},{12,13},{14,15},{16,17},{18,... | collective-permute-start | bytes 393224 | tf_op jit(solution)/shard_map/ppermute | solution.py:12
